TPU v7x, 32 devices: a whole 2x2x4 slice. The times are simulated.
32 devices in a mesh: fsdp: 8 (over y, x, core), group: 4 (over z).
Axes of the slice: x: 2, y: 2, z: 4, core: 2. Of those that a mesh axis runs over, the one named last changes fastest.
Arguments:
- gradient: bfloat16 [4, 512, 4096], P('group', 'fsdp'), may hold values from -4000 to 4000
- first_moment: bfloat16 [4, 4096, 512], P('group', 'fsdp'), may hold values from -3 to 3
- second_moment: bfloat16 [4, 4096, 512], P('group', 'fsdp'), may hold values from 0.29882812 to 3
- basis_store: bfloat16 [4, 4608, 256], P('group', 'fsdp'), may hold values from -1 to 2
- step_number: int32 [1], replicated, may hold values from 1 to 99999
- matrix_ids: int32 [4], P('group'), may hold values from 0 to 3, each once
Outputs:
- update: bfloat16 [4, 512, 4096], P('group', 'fsdp')
- new_first: bfloat16 [4, 4096, 512], P('group', 'fsdp')
- new_second: bfloat16 [4, 4096, 512], P('group', 'fsdp')
Inputs may be any that keep to these rules, and one draw needn't show every extreme that they name: `matrix_ids`: each matrix index once.
All inputs are finite; a program needn't handle non-finite values.
Results may differ from a plain program's by a relative error of at most 0.0004.
Values may be sent and summed in bfloat16 or wider, within the bound.
A program may use at most 64 MiB of HBM per device.

v0:
```python
import math
import jax
import jax.numpy as jnp
from jax import lax
from jax.sharding import PartitionSpec as P

BLOCK = 256
BETA_ONE = 0.95
BETA_TWO = 0.95
ADAM_EPS = 1e-08
HIGHEST = lax.Precision.HIGHEST


def clip_of(local_squares, entries):
    total = lax.psum(local_squares, ("fsdp", "group"))
    return jnp.float32(math.sqrt(entries)) / (jnp.sqrt(total) + 1e-06)


def local(gradient, first_moment, second_moment, basis_store, step_number, matrix_ids):
    fsdp_count = lax.axis_size("fsdp")
    group_count = lax.axis_size("group")
    row_count = gradient.shape[1]
    col_count = gradient.shape[2]
    all_rows = row_count * fsdp_count
    col_share = col_count // fsdp_count
    left_blocks = all_rows // BLOCK
    right_blocks = col_count // BLOCK
    entries = all_rows * col_count * group_count
    grad_local = gradient[0].astype(jnp.float32)
    local_squares = jnp.sum(grad_local * grad_local)
    gathered = lax.all_gather(basis_store[0], "fsdp", axis=0, tiled=True)
    owner_rows = basis_store.shape[1]
    owner = (step_number[0] + matrix_ids[0]) % fsdp_count
    ordered_half = jnp.roll(gathered, -owner * owner_rows, axis=0)
    left = ordered_half[:all_rows].astype(jnp.float32).reshape(left_blocks, BLOCK, BLOCK)
    right_half = ordered_half[all_rows:].reshape(right_blocks, BLOCK, BLOCK)
    right = right_half.astype(jnp.float32)
    turned = jnp.einsum(
        "rbj,bjl->rbl",
        gradient[0].reshape(row_count, right_blocks, BLOCK),
        right_half,
        preferred_element_type=jnp.float32,
    )
    turned = clip_of(local_squares, entries) * turned
    outgoing = turned.reshape(row_count, fsdp_count, col_share)
    received = lax.all_to_all(outgoing, "fsdp", split_axis=1, concat_axis=0, tiled=True)
    width = received.shape[2]
    columns = received[:, 0, :].reshape(left_blocks, BLOCK, width)
    rotated = jnp.einsum("bkc,bki->cbi", columns, left, precision=HIGHEST).reshape(width, all_rows)
    count = step_number[0].astype(jnp.float32)
    first_fix = 1.0 - jnp.power(jnp.float32(BETA_ONE), count)
    second_fix = 1.0 - jnp.power(jnp.float32(BETA_TWO), count)
    first_sum = BETA_ONE * first_moment[0].astype(jnp.float32) + (1.0 - BETA_ONE) * rotated
    second_sum = (
        BETA_TWO * second_moment[0].astype(jnp.float32) + (1.0 - BETA_TWO) * rotated * rotated
    )
    direction = first_sum / first_fix / (jnp.sqrt(second_sum / second_fix) + ADAM_EPS)
    backward = jnp.einsum(
        "cbi,bki->cbk", direction.reshape(col_share, left_blocks, BLOCK), left, precision=HIGHEST
    )
    returning = backward.reshape(col_share, fsdp_count, row_count)
    received = lax.all_to_all(returning, "fsdp", split_axis=1, concat_axis=0, tiled=True)
    width = received.shape[2]
    pieces = received[:, 0, :].reshape(right_blocks, BLOCK, width)
    result = jnp.einsum("blr,bjl->rbj", pieces, right, precision=HIGHEST).reshape(width, col_count)
    return (
        result[None].astype(jnp.bfloat16),
        first_sum[None].astype(jnp.bfloat16),
        second_sum[None].astype(jnp.bfloat16),
    )


def solution(mesh):
    in_specs = (
        P("group", "fsdp", None),
        P("group", "fsdp", None),
        P("group", "fsdp", None),
        P("group", "fsdp", None),
        P(),
        P("group"),
    )
    out_specs = (P("group", "fsdp", None), P("group", "fsdp", None), P("group", "fsdp", None))
    return jax.shard_map(local, mesh=mesh, in_specs=in_specs, out_specs=out_specs, check_vma=False)
```

profile of v0, /device:TPU:0, one launch (start us, length us, event | category | flops | bytes accessed | tf_op | source)
XLA Modules:
  0.0 129.9 jit_solution(4664834779437250794)
XLA Ops:
  7.2 0.0 all-gather.3.cloned.1.call-start
  7.2 0.7 all-gather.3.cloned.1.call-update
  7.9 1.9 %multiply_reduce_fusion = f32[]{:T(128)} fusion(bf16[1,64,4096]{2,1,0:T(8,128)(2,1)} %param.6), kind=kLoop, calls=%fused_computation.24 | loop fusion | flops 786431 | bytes 524292 | tf_op jit(solution)/shard_map/reduce_sum | solution.py:30
  9.8 42.2 %psum.7 = f32[]{:T(128)} all-reduce(f32[]{:T(128)} %multiply_reduce_fusion), channel_id=1, replica_groups=mesh['fsdp'=8,'group'=4] {'fsdp','group'}, use_global_device_ids=true, to_apply=%region_1.2 | all-reduce | flops 1 | bytes 8 | tf_op jit(solution)/shard_map/psum | solution.py:15
  54.0 1.1 copy.42
  55.2 0.0 all-gather.3.cloned.1.call-done
  55.3 3.7 %fusion = bf16[4608,256]{1,0:T(8,128)(2,1)S(1)} fusion(s32[]{:T(128)S(6)} %select_n.21, bf16[4608,256]{1,0:T(8,128)(2,1)} %bitcast.46), kind=kLoop, calls=%fused_computation.2 | loop fusion | flops 4718592 | bytes 4718596 | tf_op jit(solution)/shard_map/jit(_roll_dynamic)/concatenate | solution.py:34
  59.0 0.0 copy-start
  59.0 0.1 slice.8
  59.2 0.5 fusion.1
  59.6 0.8 copy-done
  60.4 0.6 copy.30
  61.0 1.3 %reshape.80 = f32[64,8,512]{2,1,0:T(8,128)} reshape(f32[64,16,256]{2,1,0:T(8,128)S(1)} %copy.30) | data formatting | bytes 2097152 | tf_op jit(solution)/shard_map/reshape | solution.py:45
  62.3 2.8 %copy.31 = f32[64,8,512]{2,0,1:T(8,128)} copy(f32[64,8,512]{2,1,0:T(8,128)} %reshape.80) | data formatting | bytes 2097152 | tf_op jit(solution)/shard_map/reshape | solution.py:45
  65.1 3.8 %all-to-all-start = ((f32[64,8,512]{2,0,1:T(8,128)}), f32[64,8,512]{2,0,1:T(8,128)S(1)}, u32[]{:S(2)}, u32[]{:S(2)}) async-start(f32[64,8,512]{2,0,1:T(8,128)} %copy.31), calls=%async_computation | async-start | bytes 2097152 | tf_op jit(solution)/shard_map/all_to_all | solution.py:46
  69.0 1.0 slice.9
  69.9 14.4 %all-to-all-done = f32[64,8,512]{2,0,1:T(8,128)S(1)} async-done(((f32[64,8,512]{2,0,1:T(8,128)}), f32[64,8,512]{2,0,1:T(8,128)S(1)}, u32[]{:S(2)}, u32[]{:S(2)}) %all-to-all-start) | async-done | bytes 1048608 | tf_op jit(solution)/shard_map/all_to_all | solution.py:46
  84.3 1.7 %fusion.23 = f32[2,256,512]{2,1,0:T(8,128)} fusion(bf16[2,256,256]{2,1,0:T(8,128)(2,1)S(1)} %bitcast.49, f32[2,256,512]{2,1,0:T(8,128)S(1)} %bitcast.43), kind=kOutput, calls=%fused_computation.32 | convolution fusion | flops 805306368 | bytes 2359296 | tf_op jit(solution)/shard_map/bkc,bki->cbi/dot_general | solution.py:49
  86.0 2.5 %copy.38 = f32[1,512,512]{2,1,0:T(8,128)} copy(f32[1,512,512]{1,2,0:T(8,128)} %bitcast.44) | data formatting | bytes 2097152 | tf_op jit(solution)/shard_map/reshape | solution.py:49
  88.6 3.0 %fusion.14 = (bf16[1,512,512]{2,1,0:T(8,128)(2,1)}, bf16[1,512,512]{2,1,0:T(8,128)(2,1)}, f32[1,512,512]{2,1,0:T(8,128)}, f32[1,512,512]{2,1,0:T(8,128)S(1)}) fusion(f32[1,512,512]{2,1,0:T(8,128)} %copy.38, bf16[1,512,512]{2,1,0:T(8,128)(2,1)} %param.8, bf16[1,512,512]{2,1,0:T(8,128)(2,1)} %param.7), kind=kLoop, calls=%fused_computation.20 | loop fusion | flops 2621440 | bytes 5242880 | tf_op jit(solution)/shard_map/convert_element_type | solution.py:69
  91.6 2.6 %copy.28 = f32[1,512,512]{1,2,0:T(8,128)} copy(f32[1,512,512]{2,1,0:T(8,128)} %get-tuple-element.5) | data formatting | bytes 2097152 | tf_op jit(solution)/shard_map/mul | solution.py:53
  94.2 1.3 %copy.33 = f32[1,512,512]{1,2,0:T(8,128)} copy(f32[1,512,512]{2,1,0:T(8,128)S(1)} %get-tuple-element.6) | data formatting | bytes 2097152 | tf_op jit(solution)/shard_map/mul | solution.py:55
  95.5 3.1 %fusion.4 = f32[2,256,512]{2,1,0:T(8,128)S(1)} fusion(bf16[2,256,256]{2,1,0:T(8,128)(2,1)S(1)} %bitcast.50, f32[512,2,256]{0,2,1:T(8,128)} %bitcast.51, f32[512,2,256]{0,2,1:T(8,128)} %bitcast.52, f32[2,256,512]{2,1,0:T(8,128)} %fusion.23, f32[]{:T(128)} %bitcast.10), kind=kOutput, calls=%fused_computation.12 | convolution fusion | flops 807403520 | bytes 4456452 | tf_op jit(solution)/shard_map/cbi,bki->cbk/dot_general | solution.py:58
  98.6 17.8 %all_to_all.30 = f32[512,8,64]{0,2,1:T(8,128)S(1)} all-to-all(f32[512,8,64]{0,2,1:T(8,128)S(1)} %bitcast.53), channel_id=1, replica_groups=mesh['fsdp'=8,'group'=4] {'fsdp'}, dimensions={1} | all-to-all | bytes 2097152 | tf_op jit(solution)/shard_map/all_to_all | solution.py:62
  116.4 1.6 %copy.35 = f32[8,512,1,64]{1,0,3,2:T(8,128)} copy(f32[8,512,1,64]{1,3,0,2:T(8,128)S(1)} %bitcast.45) | data formatting | bytes 2097152 | tf_op jit(solution)/shard_map/all_to_all | solution.py:62
  118.0 1.4 %reshape_squeeze.11 = f32[16,256,64]{1,0,2:T(8,128)S(1)} reshape(f32[8,512,1,64]{1,0,3,2:T(8,128)} %copy.35) | data formatting | bytes 2097152 | tf_op jit(solution)/shard_map/reshape;squeeze | solution.py:64
  119.4 2.3 %fusion.2 = bf16[64,16,256]{2,0,1:T(8,128)(2,1)S(1)} fusion(bf16[16,256,256]{2,1,0:T(8,128)(2,1)S(1)} %bitcast.42, f32[16,256,64]{1,0,2:T(8,128)S(1)} %reshape_squeeze.11), kind=kOutput, calls=%fused_computation.10 | convolution fusion | flops 805568512 | bytes 3670016 | tf_op jit(solution)/shard_map/blr,bjl->rbj/dot_general | solution.py:65
  121.7 0.3 copy.37
  122.0 1.0 convert_element_type.55
Async XLA Ops:
  7.2 48.1 %all-gather.3.cloned.1.call-start = ((), (), s32[]{:S(2)}) async-start(), calls=%async_computation.2 | async-start | bytes 2654208 | tf_op jit(solution)/shard_map/all_gather | solution.py:31
  59.0 1.4 %copy-start = (bf16[4608,256]{1,0:T(8,128)(2,1)}, bf16[4608,256]{1,0:T(8,128)(2,1)S(1)}, u32[]{:S(2)}) copy-start(bf16[4608,256]{1,0:T(8,128)(2,1)S(1)} %fusion) | copy-start | bytes 7077892
  65.1 19.2 %all-to-all-start = ((f32[64,8,512]{2,0,1:T(8,128)}), f32[64,8,512]{2,0,1:T(8,128)S(1)}, u32[]{:S(2)}, u32[]{:S(2)}) async-start(f32[64,8,512]{2,0,1:T(8,128)} %copy.31), calls=%async_computation | async-start | bytes 2097152 | tf_op jit(solution)/shard_map/all_to_all | solution.py:46
Sparse Core Ops, SparseCore 0:
  9.9 31.9 all-gather.2
where the time goes:
time: 131 us; the launch traced here: 130 us
  blocking collectives  60 us (46%)
  local copies, waits for them, and re-layouts  18.5 us (14%)
  between operations  16.2 us (12%)
  waiting for transfers between devices  15.1 us (12%)
  other arithmetic  8.67 us (7%)
  matrix products  7.53 us (6%)
  starting transfers between devices  3.82 us (3%)
    psum x1, blocking collectives, clip_of(): total = lax.psum(local_squares, ('fsdp', 'group'))  42.2 us
    all_to_all x1, blocking collectives, local(): lax.all_to_all(returning, 'fsdp', split_axis=1, concat_axis=0, tiled=True)  17.8 us
    all_to_all x1, waiting for transfers between devices, local(): lax.all_to_all(outgoing, 'fsdp', split_axis=1, concat_axis=0, tiled=True)  14.4 us
    reshape x2, local copies, waits for them, and re-layouts, local(): outgoing = turned.reshape(row_count, fsdp_count, col_share)  4.1 us
    all_to_all x1, starting transfers between devices, local(): lax.all_to_all(outgoing, 'fsdp', split_axis=1, concat_axis=0, tiled=True)  3.79 us
    concatenate x1, other arithmetic, local(): ordered_half = jnp.roll(gathered, -owner * owner_rows, axis=0)  3.73 us
    dot_general x1, matrix products, local(): jnp.einsum('cbi,bki->cbk', direction.reshape(col_share, left_blocks, BLOC...  3.12 us
    convert_element_type x1, other arithmetic, local(): second_sum[None].astype(jnp.bfloat16)  3.02 us
  transfers between devices with their start and end apart: 2, of which 1 were waited for; matrix products, arithmetic and copies ran while one was open for 3% of the time, Pallas kernels for 0%

commit v1 on v0

--- a/solution.py
+++ b/solution.py
@@ -9,6 +9,45 @@
 BETA_TWO = 0.95
 ADAM_EPS = 1e-08
 HIGHEST = lax.Precision.HIGHEST
+
+
+def _edit_levels_all(v0, where_dim, panel):
+    raw_out = v0.shape
+    right_arr = jnp.moveaxis(
+        v0.reshape(
+            *raw_out[:where_dim], panel, raw_out[where_dim] // panel, *raw_out[where_dim + 1 :]
+        ),
+        where_dim,
+        0,
+    )
+    return right_arr
+
+
+def convert_task_here(frame_in, array_axis):
+    frame_in = jnp.moveaxis(frame_in, 0, array_axis)
+    y = frame_in.shape
+    fresh = frame_in.reshape(
+        *y[:array_axis], y[array_axis] * y[array_axis + 1], *y[array_axis + 2 :]
+    )
+    return fresh
+
+
+def scan_sectors(axis_id, local_array, block_here, vec):
+    mixed_arr = jax.lax.axis_index(axis_id)
+    odd = jax.lax.axis_size(axis_id)
+    latest, small = (odd, mixed_arr)
+    even = _edit_levels_all(block_here, local_array, latest)
+    pages = [even[small]]
+    for tick in range(1, latest):
+        outcome_arr = even[small ^ tick]
+        kept_arr = jax.lax.ppermute(
+            outcome_arr, axis_id, [(dev_i, dev_i ^ tick) for dev_i in range(latest)]
+        )
+        pages.append(kept_arr)
+    b_next = jnp.stack(pages, axis=0)
+    even = b_next[small ^ jnp.arange(latest)]
+    field_out = convert_task_here(even, vec)
+    return field_out
 
 
 def clip_of(local_squares, entries):
@@ -59,7 +98,7 @@
         "cbi,bki->cbk", direction.reshape(col_share, left_blocks, BLOCK), left, precision=HIGHEST
     )
     returning = backward.reshape(col_share, fsdp_count, row_count)
-    received = lax.all_to_all(returning, "fsdp", split_axis=1, concat_axis=0, tiled=True)
+    received = scan_sectors("fsdp", 1, returning, 0)
     width = received.shape[2]
     pieces = received[:, 0, :].reshape(right_blocks, BLOCK, width)
     result = jnp.einsum("blr,bjl->rbj", pieces, right, precision=HIGHEST).reshape(width, col_count)

time: 131 us -> 132 us (level)
  blocking collectives: 60 us -> 42.2 us
  waiting for transfers between devices: 15.1 us -> 24.8 us
  starting transfers between devices: 3.82 us -> 8.8 us
  local copies, waits for them, and re-layouts: 18.5 us -> 23.1 us
    all_to_all x1 -> x0, blocking collectives: 17.8 us -> none  [local(): lax.all_to_all(returning, 'fsdp', split_axis=1, concat_axis=0, tiled=True)]
    ppermute x0 -> x7, waiting for transfers between devices: none -> 9.72 us  [scan_sectors(): jax.lax.ppermute(outcome_arr, axis_id, [(dev_i, dev_i ^ tick) for dev_i i...]
    ppermute x0 -> x7, starting transfers between devices: none -> 4.98 us  [scan_sectors(): jax.lax.ppermute(outcome_arr, axis_id, [(dev_i, dev_i ^ tick) for dev_i i...]
    gather x0 -> x2, local copies, waits for them, and re-layouts: none -> 3.42 us  [scan_sectors(): even = b_next[small ^ jnp.arange(latest)]]
    unnamed x3 -> x12, local copies, waits for them, and re-layouts: 1.95 us -> 3.88 us
    all_to_all x1 -> x0, local copies, waits for them, and re-layouts: 1.59 us -> none  [local(): lax.all_to_all(returning, 'fsdp', split_axis=1, concat_axis=0, tiled=True)]
  transfers between devices with their start and end apart: 2 -> 9, of which waited for: 1 -> 4; matrix products, arithmetic and copies ran while one was open for 3% -> 4% of each run, Pallas kernels for 0% -> 0%
where the time goes in v1:
time: 132 us
  blocking collectives  42.2 us (32%)
  waiting for transfers between devices  24.8 us (19%)
  local copies, waits for them, and re-layouts  23.1 us (18%)
  between operations  16.3 us (12%)
  starting transfers between devices  8.8 us (7%)
  other arithmetic  8.78 us (7%)
  matrix products  7.53 us (6%)
    psum x1, blocking collectives, clip_of(): total = lax.psum(local_squares, ('fsdp', 'group'))  42.2 us
    all_to_all x1, waiting for transfers between devices, local(): lax.all_to_all(outgoing, 'fsdp', split_axis=1, concat_axis=0, tiled=True)  14.4 us
    ppermute x7, waiting for transfers between devices, scan_sectors(): jax.lax.ppermute(outcome_arr, axis_id, [(dev_i, dev_i ^ tick) for dev_i i...  9.72 us
    ppermute x7, starting transfers between devices, scan_sectors(): jax.lax.ppermute(outcome_arr, axis_id, [(dev_i, dev_i ^ tick) for dev_i i...  4.98 us
    reshape x2, local copies, waits for them, and re-layouts, local(): outgoing = turned.reshape(row_count, fsdp_count, col_share)  4.07 us
    unnamed x12, local copies, waits for them, and re-layouts  3.88 us
    all_to_all x1, starting transfers between devices, local(): lax.all_to_all(outgoing, 'fsdp', split_axis=1, concat_axis=0, tiled=True)  3.79 us
    concatenate x1, other arithmetic, local(): ordered_half = jnp.roll(gathered, -owner * owner_rows, axis=0)  3.73 us
  transfers between devices with their start and end apart: 9, of which 4 were waited for; matrix products, arithmetic and copies ran while one was open for 4% of the time, Pallas kernels for 0%

profile of v1, /device:TPU:0, one launch (start us, length us, event | category | flops | bytes accessed | tf_op | source)
XLA Modules:
  0.0 131.5 jit_solution(7482946896449429764)
XLA Ops:
  7.2 0.0 all-gather.3.cloned.1.call-start
  7.2 0.7 all-gather.3.cloned.1.call-update
  7.9 1.9 %multiply_reduce_fusion = f32[]{:T(128)} fusion(bf16[1,64,4096]{2,1,0:T(8,128)(2,1)} %param.6), kind=kLoop, calls=%fused_computation.25 | loop fusion | flops 786431 | bytes 524292 | tf_op jit(solution)/shard_map/reduce_sum | solution.py:69
  9.8 42.2 %psum.7 = f32[]{:T(128)} all-reduce(f32[]{:T(128)} %multiply_reduce_fusion), channel_id=1, replica_groups=mesh['fsdp'=8,'group'=4] {'fsdp','group'}, use_global_device_ids=true, to_apply=%region_1.2 | all-reduce | flops 1 | bytes 8 | tf_op jit(solution)/shard_map/psum | solution.py:54
  53.3 1.1 copy.53
  55.2 0.0 all-gather.3.cloned.1.call-done
  55.3 3.7 %fusion = bf16[4608,256]{1,0:T(8,128)(2,1)S(1)} fusion(s32[]{:T(128)S(6)} %select_n.55, bf16[4608,256]{1,0:T(8,128)(2,1)} %bitcast.74), kind=kLoop, calls=%fused_computation.3 | loop fusion | flops 4718592 | bytes 4718596 | tf_op jit(solution)/shard_map/jit(_roll_dynamic)/concatenate | solution.py:73
  59.0 0.0 copy-start
  59.0 0.1 slice.10
  59.1 0.5 fusion.1
  59.6 0.8 copy-done
  60.4 0.6 copy.41
  61.0 1.3 reshape.107
  62.3 2.8 %copy.42 = f32[64,8,512]{2,0,1:T(8,128)} copy(f32[64,8,512]{2,1,0:T(8,128)} %reshape.107) | data formatting | bytes 2097152 | tf_op jit(solution)/shard_map/reshape | solution.py:84
  65.1 3.8 %all-to-all-start = ((f32[64,8,512]{2,0,1:T(8,128)}), f32[64,8,512]{2,0,1:T(8,128)S(1)}, u32[]{:S(2)}, u32[]{:S(2)}) async-start(f32[64,8,512]{2,0,1:T(8,128)} %copy.42), calls=%async_computation | async-start | bytes 2097152 | tf_op jit(solution)/shard_map/all_to_all | solution.py:85
  68.9 1.0 slice.11
  69.9 14.4 %all-to-all-done = f32[64,8,512]{2,0,1:T(8,128)S(1)} async-done(((f32[64,8,512]{2,0,1:T(8,128)}), f32[64,8,512]{2,0,1:T(8,128)S(1)}, u32[]{:S(2)}, u32[]{:S(2)}) %all-to-all-start) | async-done | bytes 1048608 | tf_op jit(solution)/shard_map/all_to_all | solution.py:85
  84.3 1.7 %fusion.24 = f32[2,256,512]{2,1,0:T(8,128)} fusion(bf16[2,256,256]{2,1,0:T(8,128)(2,1)S(1)} %bitcast.79, f32[2,256,512]{2,1,0:T(8,128)S(1)} %bitcast.72), kind=kOutput, calls=%fused_computation.51 | convolution fusion | flops 805306368 | bytes 2359296 | tf_op jit(solution)/shard_map/bkc,bki->cbi/dot_general | solution.py:88
  85.9 2.5 %copy.49 = f32[1,512,512]{2,1,0:T(8,128)} copy(f32[1,512,512]{1,2,0:T(8,128)} %bitcast.73) | data formatting | bytes 2097152 | tf_op jit(solution)/shard_map/reshape | solution.py:88
  88.5 3.1 %fusion.14 = (bf16[1,512,512]{2,1,0:T(8,128)(2,1)}, bf16[1,512,512]{2,1,0:T(8,128)(2,1)}, f32[1,512,512]{2,1,0:T(8,128)S(1)}, f32[1,512,512]{2,1,0:T(8,128)}) fusion(f32[1,512,512]{2,1,0:T(8,128)} %copy.49, bf16[1,512,512]{2,1,0:T(8,128)(2,1)} %param.8, bf16[1,512,512]{2,1,0:T(8,128)(2,1)} %param.7), kind=kLoop, calls=%fused_computation.21 | loop fusion | flops 2621440 | bytes 5242880 | tf_op jit(solution)/shard_map/convert_element_type | solution.py:108
  91.6 2.6 %copy.44 = f32[1,512,512]{1,2,0:T(8,128)} copy(f32[1,512,512]{2,1,0:T(8,128)} %get-tuple-element.13) | data formatting | bytes 2097152 | tf_op jit(solution)/shard_map/mul | solution.py:94
  94.2 1.3 %copy.39 = f32[1,512,512]{1,2,0:T(8,128)} copy(f32[1,512,512]{2,1,0:T(8,128)S(1)} %get-tuple-element.12) | data formatting | bytes 2097152 | tf_op jit(solution)/shard_map/mul | solution.py:92
  95.5 3.1 %fusion.4 = f32[2,256,512]{2,1,0:T(8,128)S(1)} fusion(bf16[2,256,256]{2,1,0:T(8,128)(2,1)S(1)} %bitcast.80, f32[512,2,256]{0,2,1:T(8,128)} %bitcast.82, f32[512,2,256]{0,2,1:T(8,128)} %bitcast.81, f32[2,256,512]{2,1,0:T(8,128)} %fusion.24, f32[]{:T(128)} %bitcast.10), kind=kOutput, calls=%fused_computation.13 | convolution fusion | flops 807403520 | bytes 4456452 | tf_op jit(solution)/shard_map/cbi,bki->cbk/dot_general | solution.py:97
  98.6 0.8 dynamic-slice_bitcast_fusion
  99.5 0.0 collective-permute-start
  99.5 0.6 collective-permute-start.1
  100.1 1.3 collective-permute-start.2
  101.3 0.6 collective-permute-start.3
  101.9 1.1 collective-permute-start.4
  103.1 0.0 collective-permute-done
  103.1 0.7 collective-permute-start.5
  103.7 0.9 bitcast_dynamic-update-slice_fusion.6
  104.6 1.4 %collective-permute-done.1 = f32[512,1,64]{0,2,1:T(8,128)S(1)} collective-permute-done((f32[512,1,64]{0,2,1:T(8,128)}, f32[512,1,64]{0,2,1:T(8,128)S(1)}, u32[]{:S(2)}, u32[]{:S(2)}) %collective-permute-start.1) | collective-permute-done | bytes 131104 | tf_op jit(solution)/shard_map/ppermute | solution.py:43
  106.1 0.8 collective-permute-start.6
  106.8 1.1 collective-permute-done.2
  108.0 0.0 collective-permute-done.3
  108.0 7.2 %collective-permute-done.4 = f32[512,1,64]{0,2,1:T(8,128)S(1)} collective-permute-done((f32[512,1,64]{0,2,1:T(8,128)S(1)}, f32[512,1,64]{0,2,1:T(8,128)S(1)}, u32[]{:S(2)}, u32[]{:S(2)}) %collective-permute-start.4) | collective-permute-done | bytes 131104 | tf_op jit(solution)/shard_map/ppermute | solution.py:43
  115.2 0.0 collective-permute-done.5
  115.2 0.0 collective-permute-done.6
  115.2 0.0 copy-start.1
  115.2 1.0 copy-done.1
  116.2 1.8 %gather_fusion = f32[8,512,64]{1,2,0:T(8,128)S(1)} fusion(f32[8,512,64]{1,2,0:T(8,128)} %bitcast.71, s32[1024]{0:T(1024)S(1)} %pad_clamp_fusion), kind=kCustom, calls=%fused_computation | custom fusion | bytes 2097184 | tf_op jit(solution)/shard_map/gather | solution.py:48
  118.1 1.6 %copy.46 = f32[8,512,64]{1,0,2:T(8,128)} copy(f32[8,512,64]{1,2,0:T(8,128)S(1)} %gather_fusion) | data formatting | bytes 2097152 | tf_op jit(solution)/shard_map/gather | solution.py:48
  119.6 1.4 %reshape_squeeze_reshape.3 = f32[16,256,64]{1,0,2:T(8,128)S(1)} reshape(f32[8,512,64]{1,0,2:T(8,128)} %copy.46) | data formatting | bytes 2097152 | tf_op jit(solution)/shard_map/reshape;squeeze;reshape | solution.py:103
  121.1 2.3 %fusion.2 = bf16[64,16,256]{2,0,1:T(8,128)(2,1)S(1)} fusion(bf16[16,256,256]{2,1,0:T(8,128)(2,1)S(1)} %bitcast.70, f32[16,256,64]{1,0,2:T(8,128)S(1)} %reshape_squeeze_reshape.3), kind=kOutput, calls=%fused_computation.11 | convolution fusion | flops 805568512 | bytes 3670016 | tf_op jit(solution)/shard_map/blr,bjl->rbj/dot_general | solution.py:104
  123.3 0.3 copy.48
  123.6 1.0 convert_element_type.55
  (9 shorter events, 0.1 us)
Async XLA Ops:
  7.2 48.1 %all-gather.3.cloned.1.call-start = ((), (), s32[]{:S(2)}) async-start(), calls=%async_computation.1 | async-start | bytes 2654208 | tf_op jit(solution)/shard_map/all_gather | solution.py:70
  59.0 1.4 %copy-start = (bf16[4608,256]{1,0:T(8,128)(2,1)}, bf16[4608,256]{1,0:T(8,128)(2,1)S(1)}, u32[]{:S(2)}) copy-start(bf16[4608,256]{1,0:T(8,128)(2,1)S(1)} %fusion) | copy-start | bytes 7077892
  65.1 19.2 %all-to-all-start = ((f32[64,8,512]{2,0,1:T(8,128)}), f32[64,8,512]{2,0,1:T(8,128)S(1)}, u32[]{:S(2)}, u32[]{:S(2)}) async-start(f32[64,8,512]{2,0,1:T(8,128)} %copy.42), calls=%async_computation | async-start | bytes 2097152 | tf_op jit(solution)/shard_map/all_to_all | solution.py:85
  99.5 3.6 %collective-permute-start = (f32[512,1,64]{0,2,1:T(8,128)}, f32[512,1,64]{0,2,1:T(8,128)}, u32[]{:S(2)}, u32[]{:S(2)}) collective-permute-start(f32[512,1,64]{0,2,1:T(8,128)} %get-tuple-element.11), channel_id=1, source_target_pairs={{0,4},{4,0},{8,12},{12,8},{16,20},{20,16},{24,28},{28,24},{1,5},{5... | collective-permute-start | bytes 393224 | tf_op jit(solution)/shard_map/ppermute | solution.py:43
  99.5 6.6 %collective-permute-start.1 = (f32[512,1,64]{0,2,1:T(8,128)}, f32[512,1,64]{0,2,1:T(8,128)S(1)}, u32[]{:S(2)}, u32[]{:S(2)}) collective-permute-start(f32[512,1,64]{0,2,1:T(8,128)} %get-tuple-element.10), channel_id=1, source_target_pairs={{0,8},{4,12},{8,0},{12,4},{16,24},{20,28},{24,16},{28,20},{1,9},{5... | collective-permute-start | bytes 393224 | tf_op jit(solution)/shard_map/ppermute | solution.py:43
  100.1 7.9 %collective-permute-start.2 = (f32[512,1,64]{0,2,1:T(8,128)}, f32[512,1,64]{0,2,1:T(8,128)S(1)}, u32[]{:S(2)}, u32[]{:S(2)}) collective-permute-start(f32[512,1,64]{0,2,1:T(8,128)} %get-tuple-element.9), channel_id=1, source_target_pairs={{0,12},{4,8},{8,4},{12,0},{16,28},{20,24},{24,20},{28,16},{1,13},{... | collective-permute-start | bytes 393224 | tf_op jit(solution)/shard_map/ppermute | solution.py:43
  101.3 6.6 %collective-permute-start.3 = (f32[512,1,64]{0,2,1:T(8,128)}, f32[512,1,64]{0,2,1:T(8,128)S(1)}, u32[]{:S(2)}, u32[]{:S(2)}) collective-permute-start(f32[512,1,64]{0,2,1:T(8,128)} %get-tuple-element.8), channel_id=1, source_target_pairs={{0,16},{4,20},{8,24},{12,28},{16,0},{20,4},{24,8},{28,12},{1,17},{... | collective-permute-start | bytes 393224 | tf_op jit(solution)/shard_map/ppermute | solution.py:43
  101.9 13.3 %collective-permute-start.4 = (f32[512,1,64]{0,2,1:T(8,128)S(1)}, f32[512,1,64]{0,2,1:T(8,128)S(1)}, u32[]{:S(2)}, u32[]{:S(2)}) collective-permute-start(f32[512,1,64]{0,2,1:T(8,128)S(1)} %get-tuple-element.7), channel_id=1, source_target_pairs={{0,20},{4,16},{8,28},{12,24},{16,4},{20,0},{24,12},{28,8},{1,21},{... | collective-permute-start | bytes 393224 | tf_op jit(solution)/shard_map/ppermute | solution.py:43
  103.1 12.1 %collective-permute-start.5 = (f32[512,1,64]{0,2,1:T(8,128)S(1)}, f32[512,1,64]{0,2,1:T(8,128)S(1)}, u32[]{:S(2)}, u32[]{:S(2)}) collective-permute-start(f32[512,1,64]{0,2,1:T(8,128)S(1)} %get-tuple-element.6), channel_id=1, source_target_pairs={{0,24},{4,28},{8,16},{12,20},{16,8},{20,12},{24,0},{28,4},{1,25},{... | collective-permute-start | bytes 393224 | tf_op jit(solution)/shard_map/ppermute | solution.py:43
  106.1 9.1 %collective-permute-start.6 = (f32[512,1,64]{0,2,1:T(8,128)S(1)}, f32[512,1,64]{0,2,1:T(8,128)S(1)}, u32[]{:S(2)}, u32[]{:S(2)}) collective-permute-start(f32[512,1,64]{0,2,1:T(8,128)S(1)} %get-tuple-element.5), channel_id=1, source_target_pairs={{0,28},{4,24},{8,20},{12,16},{16,12},{20,8},{24,4},{28,0},{1,29},{... | collective-permute-start | bytes 393224 | tf_op jit(solution)/shard_map/ppermute | solution.py:43
  115.2 1.0 copy-start.1
Sparse Core Ops, SparseCore 0:
  9.9 31.9 all-gather.2
